TPU v7x, 32 devices: a whole 2x2x4 slice. The times are simulated.
32 devices in a mesh: gx: 4 (over z), gy: 2 (over y), gz: 4 (over x, core).
Axes of the slice: x: 2, y: 2, z: 4, core: 2. Of those that a mesh axis runs over, the one named last changes fastest.
Arguments:
- adjoint_guess: float32 [2, 20, 128, 1024], P(None, 'gz', 'gy', 'gx'), may hold values from -6 to 6
- viscosity: float32 [20, 128, 1024], P('gz', 'gy', 'gx'), may hold values from 0.2 to 2
- friction: float32 [128, 1024], P('gy', 'gx'), may hold values from 0.2 to 5
- base_velocity: float32 [2, 128, 1024], P(None, 'gy', 'gx'), may hold values from -6 to 6
- surface_slope: float32 [2, 128, 1024], P(None, 'gy', 'gx'), may hold values from -6 to 6
- ice_mask: int32 [128, 1024], P('gy', 'gx'), may hold values 0 or 1
- pixel_misfit: float32 [524288], P(('gx', 'gy', 'gz')), may hold values from -6 to 6
- pixel_look: float32 [524288], P(('gx', 'gy', 'gz')), may hold values from -3.140625 to 3.140625
- pixel_tile: int32 [524288, 1], P(('gx', 'gy', 'gz')), may hold values from 0 to 7; in each aligned block of 16384 rows (0 to 16383, 16384 to 32767, ...) at most 4096 rows name the same one
- pixel_cell: int32 [524288], P(('gx', 'gy', 'gz')), may hold values from 0 to 16383
- pixel_count: int32 [32], P(('gx', 'gy', 'gz')), may hold values from 1 to 16384, 393216 in all
Outputs:
- adjoint: float32 [2, 20, 128, 1024], P(None, 'gz', 'gy', 'gx')
- sensitivity_maps: float32 [2, 128, 1024], P(None, ('gy', 'gz'), 'gx')
Inputs may be any that keep to these rules, and one draw needn't show every extreme that they name: `pixel_tile`: among the rows of one device no tile is named more than 4096 times, a bound that some block reaches. `pixel_count`: rows of a device from its count on are padding.
All inputs are finite; a program needn't handle non-finite values. No bound on the sum of `ice_mask` on one device may be relied on, other than what follows from the above.
Results may differ from a plain program's by a relative error of at most 0.00002.
Values sent between devices are 32-bit elements; how exact they have to be, the bound alone decides.
A program may use at most 128 MiB of HBM per device.

v0:
```python
import functools
import math

import jax
import jax.numpy as jnp
from jax import lax
from jax.experimental import pallas as pl
from jax.experimental.pallas import tpu as pltpu
from jax.sharding import PartitionSpec as P

GROUPS = 4
SLOT_TILES = 8
DEPTH = 1024


def lane_column(pack, lane, like):
    return jnp.broadcast_to(pack[:, lane : lane + 1], like.shape)


def from_east(value, column):
    size = value.shape[1]
    lanes = lax.broadcasted_iota(jnp.int32, value.shape, 1)
    return jnp.where(lanes == size - 1, column, pltpu.roll(value, size - 1, 1))


def from_west(value, column):
    lanes = lax.broadcasted_iota(jnp.int32, value.shape, 1)
    return jnp.where(lanes == 0, column, pltpu.roll(value, 1, 1))


def from_north(value, row):
    size = value.shape[0]
    rows = lax.broadcasted_iota(jnp.int32, value.shape, 0)
    return jnp.where(rows == size - 1, row, pltpu.roll(value, size - 1, 0))


def from_south(value, row):
    rows = lax.broadcasted_iota(jnp.int32, value.shape, 0)
    return jnp.where(rows == 0, row, pltpu.roll(value, 1, 0))


def reverse_bits(value, bits):
    out = 0
    for bit in range(bits):
        out |= ((value >> bit) & 1) << (bits - 1 - bit)
    return out


def sin_cos(angle):
    turns = jnp.floor(angle * (2.0 / math.pi) + 0.5)
    rest = angle - turns * 1.5703125
    rest = rest - turns * 4.837512969970703125e-4
    rest = rest - turns * 7.54978995489188e-8
    square = rest * rest
    sine = -1.9515295891e-4 * square + 8.3321608736e-3
    sine = (sine * square - 1.6666654611e-1) * square * rest + rest
    cosine = 2.443315711809948e-5 * square - 1.388731625493765e-3
    cosine = (cosine * square + 4.166664568298827e-2) * square * square
    cosine = cosine - 0.5 * square + 1.0
    quadrant = turns.astype(jnp.int32) & 3
    swap = (quadrant & 1) == 1
    first = jnp.where(swap, cosine, sine)
    second = jnp.where(swap, sine, cosine)
    out_sine = jnp.where(quadrant >= 2, -first, first)
    out_cosine = jnp.where((quadrant == 1) | (quadrant == 2), -second, second)
    return out_sine, out_cosine


def apply_kernel(
    counts,
    count_ref,
    misfit_ref,
    look_ref,
    tile_ref,
    cell_ref,
    guess,
    visc,
    fric,
    base,
    slope,
    mask,
    adj_out,
    maps_out,
    *scratch,
):
    nx, ny, nz = counts
    bits = nz.bit_length() - 1
    tiles = nx * ny
    layers, rows, cols = visc.shape
    size = rows // nz
    groups = GROUPS if tiles % GROUPS == 0 else 1
    per = tiles // groups
    scratch = list(scratch)
    accs = [scratch.pop(0) for _ in range(bits)]
    recvs = [scratch.pop(0) for _ in range(bits)]
    (
        pixels,
        sums,
        lhs,
        rhs,
        acc,
        tile_in,
        block,
        forcing,
        middle,
        west_edge,
        east_edge,
        south_edge,
        north_edge,
        halo_w,
        halo_e,
        halo_s,
        halo_n,
        halo_se,
        halo_nw,
        halo_d,
        halo_u,
        visc_d,
        part,
        part_in,
        edge_w,
        edge_e,
        edge_s,
        edge_n,
        ring_w,
        ring_e,
        ring_s,
        ring_n,
        ring_se,
        ring_nw,
        late,
        late_in,
        half_sem,
        tile_sem,
        last_send,
        last_recv,
        halo_sem,
        visc_sem,
        part_sem,
        ring_send,
        ring_recv,
        late_sem,
    ) = scratch
    steps, _, depth = pixels.shape[1:]
    gx, gy, gz = lax.axis_index("gx"), lax.axis_index("gy"), lax.axis_index("gz")
    tile = gx * ny + gy
    lane_step = 16
    row_step = 8
    top = nz - 1

    def remote(src, dst, send, recv, device):
        return pltpu.make_async_remote_copy(
            src_ref=src,
            dst_ref=dst,
            send_sem=send,
            recv_sem=recv,
            device_id=device,
            device_id_type=pl.DeviceIdType.MESH,
        )

    barrier = pltpu.get_barrier_semaphore()
    layer_peers = [(gx, gy, lax.rem(gz + o, nz)) for o in range(1, nz)]
    tile_peers = []
    for o in range(1, tiles):
        other = lax.rem(tile + o, tiles)
        tile_peers.append((other, (lax.div(other, ny), lax.rem(other, ny), gz)))
    for device in layer_peers + [device for _, device in tile_peers]:
        pl.semaphore_signal(barrier, inc=1, device_id=device, device_id_type=pl.DeviceIdType.MESH)

    def prepare():
        sine, cosine = sin_cos(look_ref[...])
        order = lax.broadcasted_iota(jnp.int32, misfit_ref.shape, 0) * misfit_ref.shape[1]
        order = order + lax.broadcasted_iota(jnp.int32, misfit_ref.shape, 1)
        value = jnp.where(order < count_ref[0], misfit_ref[...], 0.0)
        cell = cell_ref[...]
        row = lax.div(cell, cols)
        fields = []
        for f in (value * cosine, value * sine):
            high = f.astype(jnp.bfloat16).astype(jnp.float32)
            fields += [high, f - high]
        fields.append((tile_ref[...] * rows + row).astype(jnp.float32))
        fields.append((cell - row * cols).astype(jnp.float32))
        lanes = misfit_ref.shape[1]
        width = depth // lanes
        for f, field in enumerate(fields):
            for r in range(steps * width):
                begin = (r % width) * lanes
                pixels[f, r // width, :, begin : begin + lanes] = field[r : r + 1, :]

    starts = []
    length = nz // 2
    for bit in range(bits):
        own_bit = lax.rem(lax.div(gz, 1 << bit), 2)
        keep = own_bit * length
        give = (1 - own_bit) * length
        peer = (gx, gy, gz + (1 - 2 * own_bit) * (1 << bit))
        starts.append((keep, give, length, peer))
        length //= 2

    def half_copy(bit, g):
        _, give, length, peer = starts[bit]
        source = sums if bit == 0 else accs[bit - 1]
        own = pl.ds(g * per, per)
        return remote(
            source.at[pl.ds(give, length), own],
            recvs[bit].at[:, own],
            half_sem.at[0, bit, g],
            half_sem.at[1, bit, g],
            peer,
        )

    def bin_group(g):
        acc[...] = jnp.zeros_like(acc)

        def step(i, slot):
            if g == 0:
                ids = lax.broadcasted_iota(jnp.int32, (cols, depth), 0)
                ids = ids.astype(jnp.float32).astype(jnp.bfloat16)
                col = pixels[5, i].astype(jnp.bfloat16)
                one = jnp.ones((cols, depth), jnp.bfloat16)
                rhs[i] = jnp.where(ids == col, one, jnp.zeros_like(one))
            pieces = [pixels[f, i].astype(jnp.bfloat16) for f in range(4)]
            row = pixels[4, i]
            ids = lax.broadcasted_iota(jnp.int32, (rows, depth), 0)
            ids = ids.astype(jnp.float32).astype(jnp.bfloat16)
            zero = jnp.zeros((rows, depth), jnp.bfloat16)
            for n in range(per):
                own = (row - float((g * per + n) * rows)).astype(jnp.bfloat16)
                hit = ids == own
                for c in range(2):
                    for part_id in range(2):
                        start = ((part_id * per + n) * 2 + c) * rows
                        piece = jnp.broadcast_to(pieces[2 * c + part_id], (rows, depth))
                        lhs[slot, start : start + rows, :] = jnp.where(hit, piece, zero)
            acc[...] += lax.dot_general(
                lhs[slot], rhs[i], (((1,), (1,)), ((), ())), preferred_element_type=jnp.float32
            )

        def several(j, carry):
            for slot in range(unroll):
                step(j * unroll + slot, slot)
            return carry

        unroll = lhs.shape[0]
        lax.fori_loop(0, steps // unroll, several, 0)
        half = per * 2 * rows
        for n in range(per):
            for c in range(2):
                for q in range(nz):
                    begin = (n * 2 + c) * rows + q * size
                    sums[reverse_bits(q, bits), g * per + n, c] = (
                        acc[begin : begin + size] + acc[half + begin : half + begin + size]
                    )

    def pack(field):
        lanes = lax.broadcasted_iota(jnp.int32, (rows, 128), 1)
        west = jnp.zeros((rows, 128), jnp.float32)
        east = jnp.zeros((rows, 128), jnp.float32)
        for f in range(3):
            for k in range(layers):
                value = field[f, k] if f < 2 else visc[k]
                south_edge[f * row_step + k : f * row_step + k + 1, :] = value[0:1, :]
                north_edge[f * row_step + k : f * row_step + k + 1, :] = value[rows - 1 : rows, :]
                lane = lanes == f * lane_step + k
                west = jnp.where(lane, lane_column(value, 0, west), west)
                east = jnp.where(lane, lane_column(value, cols - 1, east), east)
        west_edge[...] = west
        east_edge[...] = east

    def halo_copies(field, turn):
        def one(index, src, dst, device):
            return remote(src, dst, halo_sem.at[turn, 0, index], halo_sem.at[turn, 1, index], device)

        return [
            (one(0, west_edge, halo_e.at[turn], (gx - 1, gy, gz)), gx > 0, gx < nx - 1),
            (one(1, east_edge, halo_w.at[turn], (gx + 1, gy, gz)), gx < nx - 1, gx > 0),
            (one(2, south_edge, halo_n.at[turn], (gx, gy - 1, gz)), gy > 0, gy < ny - 1),
            (one(3, north_edge, halo_s.at[turn], (gx, gy + 1, gz)), gy < ny - 1, gy > 0),
            (
                one(4, north_edge.at[:, 0:128], halo_se.at[turn], (gx - 1, gy + 1, gz)),
                (gx > 0) & (gy < ny - 1),
                (gx < nx - 1) & (gy > 0),
            ),
            (
                one(5, east_edge.at[0:8, :], halo_nw.at[turn], (gx + 1, gy - 1, gz)),
                (gx < nx - 1) & (gy > 0),
                (gx > 0) & (gy < ny - 1),
            ),
            (one(6, field.at[:, 0], halo_u.at[turn], (gx, gy, gz - 1)), gz > 0, gz < nz - 1),
            (one(7, field.at[:, layers - 1], halo_d.at[turn], (gx, gy, gz + 1)), gz < nz - 1, gz > 0),
        ]

    def start_all(copies):
        for copy, sends, _ in copies:

            @pl.when(sends)
            def _(copy=copy):
                copy.start()

    def wait_receives(copies):
        for copy, _, receives in copies:

            @pl.when(receives)
            def _(copy=copy):
                copy.wait_recv()

    def wait_sends(copies):
        for copy, sends, _ in copies:

            @pl.when(sends)
            def _(copy=copy):
                copy.wait_send()

    lane_ids = lax.broadcasted_iota(jnp.int32, (rows, cols), 1)
    row_ids = lax.broadcasted_iota(jnp.int32, (rows, cols), 0)

    def masks():
        mx = jnp.where((lane_ids < cols - 1) | (gx < nx - 1), 1.0, 0.0)
        my = jnp.where((row_ids < rows - 1) | (gy < ny - 1), 1.0, 0.0)
        return mx, my

    west_on = jnp.where(gx > 0, 1.0, 0.0)
    south_on = jnp.where(gy > 0, 1.0, 0.0)
    up_on = jnp.where(gz < nz - 1, 1.0, 0.0)

    def damping_of(k):
        scale = 18.0 * visc[k]
        if k == 0:
            scale = scale + jnp.where(gz == 0, fric[...], 0.0)
        return 0.6 / scale

    def west_stress(a, b, v, corner_a, corner_b, own_a, own_b, my_col):
        na = (from_north(a, corner_a) - a) * my_col
        nb = (from_north(b, corner_b) - b) * my_col
        ea = (own_a - a) * west_on
        eb = (own_b - b) * west_on
        return v * (4.0 * ea + 2.0 * nb) * west_on, v * (na + eb) * west_on

    def south_stress(a, b, v, corner_a, corner_b, own_a, own_b, mx_row):
        ea = (from_east(a, corner_a) - a) * mx_row
        eb = (from_east(b, corner_b) - b) * mx_row
        na = (own_a - a) * south_on
        nb = (own_b - b) * south_on
        return v * (4.0 * nb + 2.0 * ea) * south_on, v * (na + eb) * south_on

    def plane_image(va, vb, v, east_a, east_b, north_a, north_b, col_p, col_s, row_q, row_s, mx, my):
        ea = (from_east(va, east_a) - va) * mx
        eb = (from_east(vb, east_b) - vb) * mx
        na = (from_north(va, north_a) - va) * my
        nb = (from_north(vb, north_b) - vb) * my
        p = mx * v * (4.0 * ea + 2.0 * nb)
        q = my * v * (4.0 * nb + 2.0 * ea)
        s = v * (na + eb)
        sx = mx * s
        sy = my * s
        image_a = (from_west(p, col_p) - p) + (from_south(sy, row_s) - sy)
        image_b = (from_south(q, row_q) - q) + (from_west(sx, col_s) - sx)
        return image_a, image_b

    def sweep(field, turn, store):
        mx, my = masks()
        my_col = my[:, 0:128]
        mx_row = mx[0:8, :]
        west = jnp.where(gx > 0, halo_w[turn], 0.0)
        east = jnp.where(gx < nx - 1, halo_e[turn], 0.0)
        south = jnp.where(gy > 0, halo_s[turn], 0.0)
        north = jnp.where(gy < ny - 1, halo_n[turn], 0.0)
        corner_se = jnp.where((gx < nx - 1) & (gy > 0), halo_se[turn], 0.0)
        corner_nw = jnp.where((gx > 0) & (gy < ny - 1), halo_nw[turn], 0.0)
        own_w = west_edge[...]
        own_s = south_edge[...]
        corner_b = pltpu.roll(corner_nw, 128 - lane_step, 1)
        col_p, col_s = west_stress(
            west,
            pltpu.roll(west, 128 - lane_step, 1),
            pltpu.roll(west, 128 - 2 * lane_step, 1),
            corner_nw[0:1, :],
            corner_b[0:1, :],
            own_w,
            pltpu.roll(own_w, 128 - lane_step, 1),
            my_col,
        )
        south_a, south_b, south_v = south[0:8], south[8:16], south[16:24]
        row_q, row_s = south_stress(
            south_a,
            south_b,
            south_v,
            lane_column(corner_se[0:8], 0, south_a),
            lane_column(corner_se[8:16], 0, south_b),
            own_s[0:8],
            own_s[8:16],
            mx_row,
        )

        below_v = jnp.where(gz > 0, visc_d[...], 0.0)
        low_a = 4.0 * below_v * (field[0, 0] - jnp.where(gz > 0, halo_d[turn, 0], 0.0))
        low_b = 4.0 * below_v * (field[1, 0] - jnp.where(gz > 0, halo_d[turn, 1], 0.0))
        for k in range(layers):
            va, vb, v = field[0, k], field[1, k], visc[k]
            if k < layers - 1:
                top_a = 4.0 * v * (field[0, k + 1] - va)
                top_b = 4.0 * v * (field[1, k + 1] - vb)
            else:
                top_a = 4.0 * v * (jnp.where(gz < nz - 1, halo_u[turn, 0], 0.0) - va) * up_on
                top_b = 4.0 * v * (jnp.where(gz < nz - 1, halo_u[turn, 1], 0.0) - vb) * up_on
            image_a, image_b = plane_image(
                va,
                vb,
                v,
                lane_column(east, k, va),
                lane_column(east, lane_step + k, vb),
                north[k : k + 1],
                north[row_step + k : row_step + k + 1],
                lane_column(col_p, k, va),
                lane_column(col_s, k, va),
                row_q[k : k + 1],
                row_s[k : k + 1],
                mx,
                my,
            )
            image_a = image_a + (low_a - top_a)
            image_b = image_b + (low_b - top_b)
            if k == 0:
                basal = jnp.where(gz == 0, fric[...], 0.0)
                image_a = image_a + basal * va
                image_b = image_b + basal * vb
            low_a, low_b = top_a, top_b
            damp = damping_of(k)
            store(k, va - damp * image_a, vb - damp * image_b)

    def store_first(k, new_a, new_b):
        middle[0, k] = new_a
        middle[1, k] = new_b

    def store_second(k, new_a, new_b):
        adj_out[0, k] = new_a
        adj_out[1, k] = new_b
        term = slope[0] * new_a + slope[1] * new_b
        if k == 0:
            on_base = jnp.where(gz == 0, 1.0, 0.0)
            land = mask[...].astype(jnp.float32)
            part[0] = -on_base * land * fric[...] * (base[0] * new_a + base[1] * new_b)
            part[1] = term
        elif k < layers - 1:
            part[1] = part[1] + term
        else:
            part[1] = 0.25 * mask[...].astype(jnp.float32) * (part[1] + term)

    def tile_copy(t):
        device = (t // ny, t % ny, gz)
        return remote(
            total.at[0, t], tile_in.at[tile], tile_sem.at[0, t], tile_sem.at[1, tile], device
        )

    def finish(bit, g):
        keep, give, length, _ = starts[bit]
        source = sums if bit == 0 else accs[bit - 1]
        own = pl.ds(g * per, per)
        half_copy(bit, g).wait_recv()
        if bit + 1 < bits:
            next_keep, next_give, next_length, _ = starts[bit + 1]
            for begin in (next_give, next_keep):
                accs[bit][pl.ds(begin, next_length), own] = (
                    source[pl.ds(keep + begin, next_length), own]
                    + recvs[bit][pl.ds(begin, next_length), own]
                )
                if begin is next_give:
                    half_copy(bit + 1, g).start()
            return
        accs[bit][:, own] = source[pl.ds(keep, length), own] + recvs[bit][:, own]
        for t in range(g * per, (g + 1) * per):

            @pl.when(tile != t)
            def _(t=t):
                tile_copy(t).start()

            @pl.when(tile == t)
            def _(t=t):
                tile_in[t] = total[0, t]

    total = accs[bits - 1]

    def part_copy(o):
        device = layer_peers[o - 1]
        begin = pl.multiple_of(device[2] * size, size)
        return remote(
            part.at[:, pl.ds(begin, size), :],
            part_in.at[o - 1],
            part_sem.at[0, o - 1],
            part_sem.at[1, o - 1],
            device,
        )

    prepare()
    bin_group(0)
    pl.semaphore_wait(barrier, nz - 1 + tiles - 1)
    half_copy(0, 0).start()
    visc_up = (
        remote(visc.at[layers - 1], visc_d, visc_sem.at[0], visc_sem.at[1], (gx, gy, gz + 1)),
        gz < nz - 1,
        gz > 0,
    )
    pack(guess)
    first = halo_copies(guess, 0) + [visc_up]
    second = halo_copies(middle, 1)
    start_all(first)

    def early(turn):
        if turn == 3:
            wait_receives(first)
            wait_sends(first)
            sweep(guess, 0, store_first)
            pack(middle)
            start_all(second)
        elif turn == 5:
            wait_receives(second)
            sweep(middle, 1, store_second)
            for o in range(1, nz):
                part_copy(o).start()
            wait_sends(second)

    for turn in range(1, groups + bits):
        if turn < groups:
            bin_group(turn)
            half_copy(0, turn).start()
        for bit in reversed(range(bits)):
            g = turn - 1 - bit
            if 0 <= g < groups:
                finish(bit, g)
        early(turn)
    for turn in range(groups + bits, 3):
        early(turn)
    for t in range(tiles):

        @pl.when(tile != t)
        def _(t=t):
            remote(
                total.at[0, t], tile_in.at[t], tile_sem.at[0, t], tile_sem.at[1, t], (t // ny, t % ny, gz)
            ).wait_recv()

    own_rows = pl.ds(pl.multiple_of(gz * size, size), size)
    value = tile_in[0]
    for t in range(1, tiles):
        value = value + tile_in[t]
    land = mask[own_rows, :].astype(jnp.float32)
    value = value * land[None]
    block[...] = value

    lanes = lax.broadcasted_iota(jnp.int32, (size, 128), 1)
    west = jnp.zeros((size, 128), jnp.float32)
    east = jnp.zeros((size, 128), jnp.float32)
    for c in range(2):
        west = jnp.where(lanes == c * lane_step, lane_column(value[c], 0, west), west)
        east = jnp.where(lanes == c * lane_step, lane_column(value[c], cols - 1, east), east)
        edge_s[c * row_step : c * row_step + 1, :] = value[c, 0:1, :]
        edge_n[c * row_step : c * row_step + 1, :] = value[c, size - 1 : size, :]
    edge_w[...] = west
    edge_e[...] = east

    is_top = gz == top
    low = gz == 0

    def ring_one(index, src, dst, slot, device):
        return remote(src, dst, ring_send.at[index], ring_recv.at[slot], device)

    def ring_column(index, src, ring, q, device, slot):
        return ring_one(index, src, ring.at[q], slot, device)

    ring_sends = [
        (ring_one(0, edge_w, ring_e.at[gz], gz, (gx - 1, gy, top)), gx > 0),
        (ring_one(1, edge_e, ring_w.at[gz], nz + gz, (gx + 1, gy, top)), gx < nx - 1),
        (ring_one(2, edge_s, ring_n, 2 * nz, (gx, gy - 1, top)), low & (gy > 0)),
        (ring_one(3, edge_n, ring_s, 2 * nz + 1, (gx, gy + 1, top)), is_top & (gy < ny - 1)),
        (
            ring_one(4, edge_n.at[:, 0:128], ring_se, 2 * nz + 2, (gx - 1, gy + 1, top)),
            is_top & (gx > 0) & (gy < ny - 1),
        ),
        (
            ring_one(5, edge_e.at[0:8, :], ring_nw, 2 * nz + 3, (gx + 1, gy - 1, top)),
            low & (gx < nx - 1) & (gy > 0),
        ),
    ]
    for copy, sends in ring_sends:

        @pl.when(sends)
        def _(copy=copy):
            copy.start()

    to_last = remote(block, forcing.at[gz], last_send, last_recv.at[gz], (gx, gy, top))

    @pl.when(gz < top)
    def _():
        to_last.start()

    def late_copy(j):
        return remote(late.at[j], late_in, late_sem.at[0, j], late_sem.at[1, 0], (gx, gy, j))

    gathered = part[:, own_rows, :]
    for o in range(1, nz):
        part_copy(o).wait_recv()
        gathered = gathered + part_in[o - 1]
    maps_out[...] = gathered

    @pl.when(is_top)
    def _():
        forcing[top] = block[...]
        for j in range(top):
            remote(block, forcing.at[j], last_send, last_recv.at[j], (gx, gy, 0)).wait_recv()
        peer = (lax.rem(gx + 1, nx), gy, top)
        for j in range(nz):

            @pl.when(gx < nx - 1)
            def _(j=j):
                ring_one(0, edge_w, ring_e.at[j], j, peer).wait_recv()

            @pl.when(gx > 0)
            def _(j=j):
                ring_one(1, edge_e, ring_w.at[j], nz + j, peer).wait_recv()

        @pl.when(gy < ny - 1)
        def _():
            ring_one(2, edge_s, ring_n, 2 * nz, peer).wait_recv()

        @pl.when(gy > 0)
        def _():
            ring_one(3, edge_n, ring_s, 2 * nz + 1, peer).wait_recv()

        @pl.when((gx < nx - 1) & (gy > 0))
        def _():
            ring_one(4, edge_n.at[:, 0:128], ring_se, 2 * nz + 2, peer).wait_recv()

        @pl.when((gx > 0) & (gy < ny - 1))
        def _():
            ring_one(5, edge_e.at[0:8, :], ring_nw, 2 * nz + 3, peer).wait_recv()

        mx, my = masks()
        my_col = my[:, 0:128]
        mx_row = mx[0:8, :]
        last = layers - 1
        shift = 128 - 2 * lane_step - last

        def scaled(on, force, v):
            return jnp.where(on, force * (0.6 / (18.0 * v)), 0.0)

        def columns(value):
            a = lane_column(value, 0, value)
            return a, lane_column(value, lane_step, value)

        v = visc[last]
        damp = damping_of(last)
        force_a = jnp.concatenate([forcing[q, 0] for q in range(nz)], axis=0)
        force_b = jnp.concatenate([forcing[q, 1] for q in range(nz)], axis=0)
        ea = damp * force_a
        eb = damp * force_b

        west_v = lane_column(halo_w[0], 2 * lane_step + last, halo_w[0])
        east_v = lane_column(halo_e[0], 2 * lane_step + last, halo_e[0])
        south_v = jnp.broadcast_to(halo_s[0, 16 + last : 17 + last, :], (8, cols))
        north_v = jnp.broadcast_to(halo_n[0, 16 + last : 17 + last, :], (8, cols))
        nw_v = lane_column(halo_nw[0], 2 * lane_step + last, halo_nw[0])
        se_v = jnp.broadcast_to(halo_se[0, 16 + last : 17 + last, :], (8, 128))

        ring_w_all = jnp.concatenate([ring_w[q] for q in range(nz)], axis=0)
        ring_e_all = jnp.concatenate([ring_e[q] for q in range(nz)], axis=0)
        west_a, west_b = [scaled(gx > 0, f, west_v) for f in columns(ring_w_all)]
        east_a, east_b = [scaled(gx < nx - 1, f, east_v) for f in columns(ring_e_all)]
        nw_on = (gx > 0) & (gy < ny - 1)
        se_on = (gx < nx - 1) & (gy > 0)
        nw_a, nw_b = [scaled(nw_on, f, nw_v) for f in columns(ring_nw[...])]
        south_a = scaled(gy > 0, ring_s[0:8], south_v)
        south_b = scaled(gy > 0, ring_s[8:16], south_v)
        north_a = scaled(gy < ny - 1, ring_n[0:8], north_v)
        north_b = scaled(gy < ny - 1, ring_n[8:16], north_v)
        se_a = scaled(se_on, ring_se[0:8], se_v)
        se_b = scaled(se_on, ring_se[8:16], se_v)
        west_v = jnp.where(gx > 0, west_v, 0.0)
        south_v = jnp.where(gy > 0, south_v, 0.0)

        col_p, col_s = west_stress(
            west_a,
            west_b,
            west_v,
            nw_a[0:1, :],
            nw_b[0:1, :],
            lane_column(ea, 0, west_a),
            lane_column(eb, 0, west_b),
            my_col,
        )
        row_q, row_s = south_stress(
            south_a,
            south_b,
            south_v,
            lane_column(se_a, 0, south_a),
            lane_column(se_b, 0, south_b),
            jnp.broadcast_to(ea[0:1, :], south_a.shape),
            jnp.broadcast_to(eb[0:1, :], south_b.shape),
            mx_row,
        )
        image_a, image_b = plane_image(
            ea,
            eb,
            v,
            lane_column(east_a, 0, ea),
            lane_column(east_b, 0, eb),
            north_a[0:1],
            north_b[0:1],
            lane_column(col_p, 0, ea),
            lane_column(col_s, 0, ea),
            row_q[0:1],
            row_s[0:1],
            mx,
            my,
        )
        below = 4.0 * visc[last - 1]
        image_a = image_a + below * ea
        image_b = image_b + below * eb
        top_a = ea + damp * (force_a - image_a)
        top_b = eb + damp * (force_b - image_b)
        lift = damping_of(last - 1) * below
        low_a = lift * ea
        low_b = lift * eb
        land = mask[...].astype(jnp.float32)
        drive = 0.25 * land * (slope[0] * (top_a + low_a) + slope[1] * (top_b + low_b))
        for j in range(nz):
            late[j] = drive[j * size : (j + 1) * size, :]
        for j in range(top):
            late_copy(j).start()
        adj_out[0, last] = adj_out[0, last] + top_a
        adj_out[1, last] = adj_out[1, last] + top_b
        adj_out[0, last - 1] = adj_out[0, last - 1] + low_a
        adj_out[1, last - 1] = adj_out[1, last - 1] + low_b
        maps_out[1] = maps_out[1] + late[top]
        for j in range(top):
            late_copy(j).wait_send()

    @pl.when(gz < top)
    def _():
        remote(late.at[0], late_in, late_sem.at[0, 0], late_sem.at[1, 0], (gx, gy, top)).wait_recv()
        maps_out[1] = maps_out[1] + late_in[...]

    for bit in range(bits):
        for g in range(groups):
            half_copy(bit, g).wait_send()
    for t in range(tiles):

        @pl.when(tile != t)
        def _(t=t):
            tile_copy(t).wait_send()

    @pl.when(gz < top)
    def _():
        to_last.wait_send()

    for copy, sends in ring_sends:

        @pl.when(sends)
        def _(copy=copy):
            copy.wait_send()

    for o in range(1, nz):
        part_copy(o).wait_send()


def apply_twice(count, pixels, guess, visc, fric, base, slope, mask, counts):
    nx, ny, nz = counts
    tiles = nx * ny
    bits = nz.bit_length() - 1
    _, layers, rows, cols = guess.shape
    size = rows // nz
    f32 = jnp.float32
    groups = GROUPS if tiles % GROUPS == 0 else 1
    per = tiles // groups
    per_device = pixels[0].shape[0]
    depth = min(DEPTH, per_device)
    steps = per_device // depth
    flat = [value.reshape(per_device // 128, 128) for value in pixels]
    slots = math.gcd(steps, max(1, SLOT_TILES // per))
    halves = [pltpu.VMEM((nz >> (bit + 1), tiles, 2, size, cols), f32) for bit in range(bits)]
    vmem = pl.BlockSpec(memory_space=pltpu.VMEM)
    dma = pltpu.SemaphoreType.DMA
    return pl.pallas_call(
        functools.partial(apply_kernel, counts),
        in_specs=[pl.BlockSpec(memory_space=pltpu.SMEM)] + [vmem] * 10,
        out_specs=(vmem, vmem),
        out_shape=(pltpu.VMEM(guess.shape, f32), pltpu.VMEM((2, size, cols), f32)),
        scratch_shapes=halves
        + halves
        + [
            pltpu.VMEM((6, steps, 1, depth), f32),
            pltpu.VMEM((nz, tiles, 2, size, cols), f32),
            pltpu.VMEM((slots, per * 4 * rows, depth), jnp.bfloat16),
            pltpu.VMEM((steps, cols, depth), jnp.bfloat16),
            pltpu.VMEM((per * 4 * rows, cols), f32),
            pltpu.VMEM((tiles, 2, size, cols), f32),
            pltpu.VMEM((2, size, cols), f32),
            pltpu.VMEM((nz, 2, size, cols), f32),
            pltpu.VMEM(guess.shape, f32),
            pltpu.VMEM((rows, 128), f32),
            pltpu.VMEM((rows, 128), f32),
            pltpu.VMEM((24, cols), f32),
            pltpu.VMEM((24, cols), f32),
            pltpu.VMEM((2, rows, 128), f32),
            pltpu.VMEM((2, rows, 128), f32),
            pltpu.VMEM((2, 24, cols), f32),
            pltpu.VMEM((2, 24, cols), f32),
            pltpu.VMEM((2, 24, 128), f32),
            pltpu.VMEM((2, 8, 128), f32),
            pltpu.VMEM((2, 2, rows, cols), f32),
            pltpu.VMEM((2, 2, rows, cols), f32),
            pltpu.VMEM((rows, cols), f32),
            pltpu.VMEM((2, rows, cols), f32),
            pltpu.VMEM((nz - 1, 2, size, cols), f32),
            pltpu.VMEM((size, 128), f32),
            pltpu.VMEM((size, 128), f32),
            pltpu.VMEM((16, cols), f32),
            pltpu.VMEM((16, cols), f32),
            pltpu.VMEM((nz, size, 128), f32),
            pltpu.VMEM((nz, size, 128), f32),
            pltpu.VMEM((16, cols), f32),
            pltpu.VMEM((16, cols), f32),
            pltpu.VMEM((16, 128), f32),
            pltpu.VMEM((8, 128), f32),
            pltpu.VMEM((nz, size, cols), f32),
            pltpu.VMEM((size, cols), f32),
            dma((2, bits, groups)),
            dma((2, tiles)),
            dma,
            dma((nz,)),
            dma((2, 2, 8)),
            dma((2,)),
            dma((2, nz - 1)),
            dma((6,)),
            dma((2 * nz + 4,)),
            dma((2, nz)),
        ],
        compiler_params=pltpu.CompilerParams(
            collective_id=0, has_side_effects=True, vmem_limit_bytes=56 * 2**20
        ),
        name="apply_twice",
    )(count, *flat, guess, visc, fric, base, slope, mask)


def body(
    adjoint_guess,
    viscosity,
    friction,
    base_velocity,
    surface_slope,
    ice_mask,
    pixel_misfit,
    pixel_look,
    pixel_tile,
    pixel_cell,
    pixel_count,
):
    sizes = tuple(lax.axis_size(name) for name in ("gx", "gy", "gz"))
    pixels = (pixel_misfit, pixel_look, pixel_tile[:, 0], pixel_cell)
    return apply_twice(
        pixel_count,
        pixels,
        adjoint_guess,
        viscosity,
        friction,
        base_velocity,
        surface_slope,
        ice_mask,
        sizes,
    )


def solution(mesh):
    return jax.shard_map(
        body,
        mesh=mesh,
        in_specs=(
            P(None, "gz", "gy", "gx"),
            P("gz", "gy", "gx"),
            P("gy", "gx"),
            P(None, "gy", "gx"),
            P(None, "gy", "gx"),
            P("gy", "gx"),
            P(("gx", "gy", "gz")),
            P(("gx", "gy", "gz")),
            P(("gx", "gy", "gz"), None),
            P(("gx", "gy", "gz")),
            P(("gx", "gy", "gz")),
        ),
        out_specs=(P(None, "gz", "gy", "gx"), P(None, ("gy", "gz"), "gx")),
        check_vma=False,
    )
```

profile of v0, /device:TPU:21, one launch (start us, length us, event | category | flops | bytes accessed | tf_op | source)
XLA Modules:
  0.0 43.9 jit_solution(8069503047017134345)
XLA Ops:
  1.3 41.2 %apply_twice.1 = (f32[2,5,64,256]{3,2,1,0:T(8,128)S(1)}, f32[2,16,256]{2,1,0:T(8,128)S(1)}) custom-call(s32[1]{0:T(128)S(6)} %copy.17.count_ref, f32[128,128]{1,0:T(8,128)} %bitcast.4, f32[128,128]{1,0:T(8,128)} %bitcast.5, s32[128,128]{1,0:T(8,128)} %bitcast.6, s32[128,128]{1,0:T(8,128)} %bitcast.7, f32[2,5,64,256]{3,2,1,0:T(8,128)} %guess.1, ...), custom_call_target="tpu_custom_call" | custom-call | tf_op jit(solution)/shard_map/apply_twice/pallas_call | solution.py:781
  42.5 0.8 %copy.15 = f32[2,5,64,256]{3,2,1,0:T(8,128)} copy(f32[2,5,64,256]{3,2,1,0:T(8,128)S(1)} %get-tuple-element.2) | data formatting | bytes 1310720
  43.3 0.6 %copy.16 = f32[2,16,256]{2,1,0:T(8,128)} copy(f32[2,16,256]{2,1,0:T(8,128)S(1)} %get-tuple-element.3) | data formatting | bytes 65536
where the time goes:
time: 44.7 us; the launch traced here: 43.9 us
  Pallas kernels  41.2 us (92%)
  local copies, waits for them, and re-layouts  1.45 us (3%)
  between operations  1.29 us (3%)
    pallas_call x1, Pallas kernels, apply_twice(): pl.pallas_call(functools.partial(apply_kernel, counts), in_specs=[pl.Bloc...  41.2 us
    unnamed x2, local copies, waits for them, and re-layouts  1.45 us

commit v1 on v0

--- a/solution.py
+++ b/solution.py
@@ -8,9 +8,8 @@
 from jax.experimental.pallas import tpu as pltpu
 from jax.sharding import PartitionSpec as P
 
-GROUPS = 4
-SLOT_TILES = 8
-DEPTH = 1024
+SHARES = (3, 2, 2, 1)
+FIRST = -1
 
 
 def lane_column(pack, lane, like):
@@ -64,6 +63,79 @@
     out_sine = jnp.where(quadrant >= 2, -first, first)
     out_cosine = jnp.where((quadrant == 1) | (quadrant == 2), -second, second)
     return out_sine, out_cosine
+
+
+def exchange(words, bit, inner):
+    blocks, sublanes, lanes = words[0].shape
+    vregs = inner.bit_length() - 1
+    if bit < vregs or bit >= vregs + 10:
+        half = 1 << bit if bit < vregs else inner
+        shape = (blocks // (2 * half), 2, half, sublanes, lanes)
+        parts = [word.reshape(shape) for word in words]
+        lower = [part[:, 0] for part in parts]
+        upper = [part[:, 1] for part in parts]
+        swap = lower[0] > upper[0]
+        out = []
+        for a, b in zip(lower, upper):
+            first = jnp.where(swap, b, a)
+            second = jnp.where(swap, a, b)
+            out.append(jnp.stack([first, second], axis=1).reshape(blocks, sublanes, lanes))
+        return out
+    axis = 1 if bit < vregs + 3 else 2
+    step = 1 << (bit - vregs) if axis == 1 else 1 << (bit - vregs - 3)
+    size = (sublanes, lanes)[axis - 1]
+    spots = lax.broadcasted_iota(jnp.int32, (1, sublanes, lanes), axis)
+    high = jnp.broadcast_to((spots & step) != 0, words[0].shape)
+    sign = jnp.where((spots & step) != 0, -1.0, 1.0)
+    partners = []
+    for word in words:
+        back = pltpu.roll(word, step, axis)
+        if 2 * step == size:
+            partners.append(back)
+        else:
+            partners.append(jnp.where(high, back, pltpu.roll(word, size - step, axis)))
+    take = (partners[0] - words[0]) * sign < 0.0
+    return [jnp.where(take, partner, word) for partner, word in zip(partners, words)]
+
+
+def order_bit(shape, bit):
+    vregs = shape[0].bit_length() - 1
+    if bit < vregs:
+        return lax.broadcasted_iota(jnp.int32, shape, 0) & (1 << bit)
+    if bit < vregs + 3:
+        return lax.broadcasted_iota(jnp.int32, shape, 1) & (1 << (bit - vregs))
+    return lax.broadcasted_iota(jnp.int32, shape, 2) & (1 << (bit - vregs - 3))
+
+
+def order_of(shape):
+    block = lax.broadcasted_iota(jnp.int32, shape, 0)
+    row = lax.broadcasted_iota(jnp.int32, shape, 1)
+    lane = lax.broadcasted_iota(jnp.int32, shape, 2)
+    return (lane * shape[1] + row) * shape[0] + block
+
+
+def sort_words(words):
+    shape = words[0].shape
+    bits = math.prod(shape).bit_length() - 1
+    key, rest = words[0], list(words[1:])
+    sign = None
+    for phase in range(1, bits + 1):
+        after = 1.0
+        if phase < bits:
+            after = jnp.where(order_bit(shape, phase) != 0, -1.0, 1.0)
+        turn = after if sign is None else after * sign
+        key = key * turn
+        sign = after
+        for bit in reversed(range(phase)):
+            key, *rest = exchange([key] + rest, bit, shape[0])
+    return [key] + rest
+
+
+def tile_spans(tiles):
+    if tiles % sum(SHARES):
+        return [(0, tiles)]
+    unit = tiles // sum(SHARES)
+    return [(sum(SHARES[:g]) * unit, share * unit) for g, share in enumerate(SHARES)]
 
 
 def apply_kernel(
@@ -88,8 +160,8 @@
     tiles = nx * ny
     layers, rows, cols = visc.shape
     size = rows // nz
-    groups = GROUPS if tiles % GROUPS == 0 else 1
-    per = tiles // groups
+    spans = tile_spans(tiles)
+    groups = len(spans)
     scratch = list(scratch)
     accs = [scratch.pop(0) for _ in range(bits)]
     recvs = [scratch.pop(0) for _ in range(bits)]
@@ -141,7 +213,7 @@
         ring_recv,
         late_sem,
     ) = scratch
-    steps, _, depth = pixels.shape[1:]
+    chunks, chunk_rows = pixels.shape[1] // tiles, pixels.shape[2]
     gx, gy, gz = lax.axis_index("gx"), lax.axis_index("gy"), lax.axis_index("gz")
     tile = gx * ny + gy
     lane_step = 16
@@ -172,20 +244,41 @@
         order = lax.broadcasted_iota(jnp.int32, misfit_ref.shape, 0) * misfit_ref.shape[1]
         order = order + lax.broadcasted_iota(jnp.int32, misfit_ref.shape, 1)
         value = jnp.where(order < count_ref[0], misfit_ref[...], 0.0)
-        cell = cell_ref[...]
-        row = lax.div(cell, cols)
-        fields = []
-        for f in (value * cosine, value * sine):
-            high = f.astype(jnp.bfloat16).astype(jnp.float32)
-            fields += [high, f - high]
-        fields.append((tile_ref[...] * rows + row).astype(jnp.float32))
-        fields.append((cell - row * cols).astype(jnp.float32))
-        lanes = misfit_ref.shape[1]
-        width = depth // lanes
-        for f, field in enumerate(fields):
-            for r in range(steps * width):
-                begin = (r % width) * lanes
-                pixels[f, r // width, :, begin : begin + lanes] = field[r : r + 1, :]
+        total_rows, lanes = misfit_ref.shape
+        cells = rows * cols
+        cap = chunks * chunk_rows * lanes
+        names = tile_ref[...]
+        key = (names * cells + cell_ref[...]).astype(jnp.float32)
+        shape = (total_rows // 8, 8, lanes)
+        words = [word.reshape(shape) for word in (key, value * cosine, value * sine)]
+        words = sort_words(words)
+        place = total_rows * lanes - 1 - order_of(shape)
+        filler = jnp.zeros(shape, jnp.float32)
+        for t in range(tiles - 1):
+            below = jnp.where(names <= t, 1.0, 0.0)
+            below = jnp.sum(jnp.sum(below, axis=0, keepdims=True), axis=1, keepdims=True)
+            spare = (float(cap * (t + 1)) - below).reshape(1, 1, 1)
+            filler = filler + jnp.where(place.astype(jnp.float32) >= spare, float(cells), 0.0)
+        zero = jnp.zeros(shape, jnp.float32)
+        words = [jnp.concatenate(pair, axis=0) for pair in zip(words, (filler, zero, zero))]
+        for bit in reversed(range((total_rows * lanes).bit_length())):
+            words = exchange(words, bit, shape[0])
+        width = chunk_rows
+        for side in range(2):
+            half = slice(side * shape[0], (side + 1) * shape[0])
+            key, fx, fy = [word[half].reshape(total_rows, lanes).T for word in words]
+            spots = lax.broadcasted_iota(jnp.int32, (lanes, total_rows), 0) + side * lanes
+            owner = lax.div(spots * total_rows, cap).astype(jnp.float32)
+            cell = key - owner * float(cells)
+            row = jnp.floor((cell + 0.5) * (1.0 / cols))
+            fields = []
+            for f in (fx, fy):
+                high = f.astype(jnp.bfloat16).astype(jnp.float32)
+                fields += [high, f - high]
+            fields += [row, cell - row * float(cols)]
+            for f, field in enumerate(fields):
+                for r in range(lanes // width):
+                    pixels[f, side * (lanes // width) + r] = field[r * width : (r + 1) * width, :]
 
     starts = []
     length = nz // 2
@@ -200,7 +293,7 @@
     def half_copy(bit, g):
         _, give, length, peer = starts[bit]
         source = sums if bit == 0 else accs[bit - 1]
-        own = pl.ds(g * per, per)
+        own = pl.ds(*spans[g])
         return remote(
             source.at[pl.ds(give, length), own],
             recvs[bit].at[:, own],
@@ -210,47 +303,50 @@
         )
 
     def bin_group(g):
-        acc[...] = jnp.zeros_like(acc)
-
-        def step(i, slot):
-            if g == 0:
-                ids = lax.broadcasted_iota(jnp.int32, (cols, depth), 0)
-                ids = ids.astype(jnp.float32).astype(jnp.bfloat16)
-                col = pixels[5, i].astype(jnp.bfloat16)
-                one = jnp.ones((cols, depth), jnp.bfloat16)
-                rhs[i] = jnp.where(ids == col, one, jnp.zeros_like(one))
-            pieces = [pixels[f, i].astype(jnp.bfloat16) for f in range(4)]
-            row = pixels[4, i]
-            ids = lax.broadcasted_iota(jnp.int32, (rows, depth), 0)
+        def build(i, slot):
+            ids = lax.broadcasted_iota(jnp.int32, (cols, 128), 0)
             ids = ids.astype(jnp.float32).astype(jnp.bfloat16)
-            zero = jnp.zeros((rows, depth), jnp.bfloat16)
-            for n in range(per):
-                own = (row - float((g * per + n) * rows)).astype(jnp.bfloat16)
-                hit = ids == own
-                for c in range(2):
-                    for part_id in range(2):
-                        start = ((part_id * per + n) * 2 + c) * rows
-                        piece = jnp.broadcast_to(pieces[2 * c + part_id], (rows, depth))
-                        lhs[slot, start : start + rows, :] = jnp.where(hit, piece, zero)
-            acc[...] += lax.dot_general(
-                lhs[slot], rhs[i], (((1,), (1,)), ((), ())), preferred_element_type=jnp.float32
-            )
-
-        def several(j, carry):
-            for slot in range(unroll):
-                step(j * unroll + slot, slot)
-            return carry
-
-        unroll = lhs.shape[0]
-        lax.fori_loop(0, steps // unroll, several, 0)
-        half = per * 2 * rows
-        for n in range(per):
+            row_ids = lax.broadcasted_iota(jnp.int32, (rows, 128), 0)
+            row_ids = row_ids.astype(jnp.float32).astype(jnp.bfloat16)
+            one = jnp.ones((cols, 128), jnp.bfloat16)
+            none = jnp.zeros((cols, 128), jnp.bfloat16)
+            zero = jnp.zeros((rows, 128), jnp.bfloat16)
+            fields = [pixels[f, i] for f in range(6)]
+
+            def spread(field, j, length):
+                strip = jnp.broadcast_to(field[j : j + 1, :], (16, 128)).astype(jnp.bfloat16)
+                return jnp.concatenate([strip] * (length // 16), axis=0)
+
+            for j in range(chunk_rows):
+                span = slice(j * 128, (j + 1) * 128)
+                rhs[slot, :, span] = jnp.where(ids == spread(fields[5], j, cols), one, none)
+                hit = row_ids == spread(fields[4], j, rows)
+                for f in range(4):
+                    start = ((f % 2) * 2 + f // 2) * rows
+                    piece = spread(fields[f], j, rows)
+                    lhs[slot, start : start + rows, span] = jnp.where(hit, piece, zero)
+
+        def one_tile(n, carry):
+            t = spans[g][0] + n
+            for slot in range(chunks):
+                build(t * chunks + slot, slot)
+                product = lax.dot_general(
+                    lhs[slot], rhs[slot], (((1,), (1,)), ((), ())), preferred_element_type=jnp.float32
+                )
+                if slot == 0:
+                    acc[...] = product
+                else:
+                    acc[...] += product
+            half = 2 * rows
             for c in range(2):
                 for q in range(nz):
-                    begin = (n * 2 + c) * rows + q * size
-                    sums[reverse_bits(q, bits), g * per + n, c] = (
+                    begin = c * rows + q * size
+                    sums[reverse_bits(q, bits), t, c] = (
                         acc[begin : begin + size] + acc[half + begin : half + begin + size]
                     )
+            return carry
+
+        lax.fori_loop(0, spans[g][1], one_tile, 0)
 
     def pack(field):
         lanes = lax.broadcasted_iota(jnp.int32, (rows, 128), 1)
@@ -455,7 +551,7 @@
     def finish(bit, g):
         keep, give, length, _ = starts[bit]
         source = sums if bit == 0 else accs[bit - 1]
-        own = pl.ds(g * per, per)
+        own = pl.ds(*spans[g])
         half_copy(bit, g).wait_recv()
         if bit + 1 < bits:
             next_keep, next_give, next_length, _ = starts[bit + 1]
@@ -468,7 +564,7 @@
                     half_copy(bit + 1, g).start()
             return
         accs[bit][:, own] = source[pl.ds(keep, length), own] + recvs[bit][:, own]
-        for t in range(g * per, (g + 1) * per):
+        for t in range(spans[g][0], sum(spans[g])):
 
             @pl.when(tile != t)
             def _(t=t):
@@ -506,13 +602,13 @@
     start_all(first)
 
     def early(turn):
-        if turn == 3:
+        if turn == groups + FIRST:
             wait_receives(first)
             wait_sends(first)
             sweep(guess, 0, store_first)
             pack(middle)
             start_all(second)
-        elif turn == 5:
+        elif turn == groups + bits - 1:
             wait_receives(second)
             sweep(middle, 1, store_second)
             for o in range(1, nz):
@@ -527,8 +623,6 @@
             g = turn - 1 - bit
             if 0 <= g < groups:
                 finish(bit, g)
-        early(turn)
-    for turn in range(groups + bits, 3):
         early(turn)
     for t in range(tiles):
 
@@ -594,12 +688,6 @@
 
     def late_copy(j):
         return remote(late.at[j], late_in, late_sem.at[0, j], late_sem.at[1, 0], (gx, gy, j))
-
-    gathered = part[:, own_rows, :]
-    for o in range(1, nz):
-        part_copy(o).wait_recv()
-        gathered = gathered + part_in[o - 1]
-    maps_out[...] = gathered
 
     @pl.when(is_top)
     def _():
@@ -729,14 +817,23 @@
         adj_out[1, last] = adj_out[1, last] + top_b
         adj_out[0, last - 1] = adj_out[0, last - 1] + low_a
         adj_out[1, last - 1] = adj_out[1, last - 1] + low_b
-        maps_out[1] = maps_out[1] + late[top]
         for j in range(top):
             late_copy(j).wait_send()
+
+    gathered = part[:, own_rows, :]
+    for o in range(1, nz):
+        part_copy(o).wait_recv()
+        gathered = gathered + part_in[o - 1]
+    maps_out[0] = gathered[0]
+
+    @pl.when(is_top)
+    def _():
+        maps_out[1] = gathered[1] + late[top]
 
     @pl.when(gz < top)
     def _():
         remote(late.at[0], late_in, late_sem.at[0, 0], late_sem.at[1, 0], (gx, gy, top)).wait_recv()
-        maps_out[1] = maps_out[1] + late_in[...]
+        maps_out[1] = gathered[1] + late_in[...]
 
     for bit in range(bits):
         for g in range(groups):
@@ -768,13 +865,13 @@
     _, layers, rows, cols = guess.shape
     size = rows // nz
     f32 = jnp.float32
-    groups = GROUPS if tiles % GROUPS == 0 else 1
-    per = tiles // groups
+    groups = len(tile_spans(tiles))
     per_device = pixels[0].shape[0]
-    depth = min(DEPTH, per_device)
-    steps = per_device // depth
+    cap = 2 * per_device // tiles
+    chunk_rows = min(8, cap // 128)
+    depth = chunk_rows * 128
+    chunks = cap // depth
     flat = [value.reshape(per_device // 128, 128) for value in pixels]
-    slots = math.gcd(steps, max(1, SLOT_TILES // per))
     halves = [pltpu.VMEM((nz >> (bit + 1), tiles, 2, size, cols), f32) for bit in range(bits)]
     vmem = pl.BlockSpec(memory_space=pltpu.VMEM)
     dma = pltpu.SemaphoreType.DMA
@@ -786,11 +883,11 @@
         scratch_shapes=halves
         + halves
         + [
-            pltpu.VMEM((6, steps, 1, depth), f32),
+            pltpu.VMEM((6, tiles * chunks, chunk_rows, 128), f32),
             pltpu.VMEM((nz, tiles, 2, size, cols), f32),
-            pltpu.VMEM((slots, per * 4 * rows, depth), jnp.bfloat16),
-            pltpu.VMEM((steps, cols, depth), jnp.bfloat16),
-            pltpu.VMEM((per * 4 * rows, cols), f32),
+            pltpu.VMEM((chunks, 4 * rows, depth), jnp.bfloat16),
+            pltpu.VMEM((chunks, cols, depth), jnp.bfloat16),
+            pltpu.VMEM((4 * rows, cols), f32),
             pltpu.VMEM((tiles, 2, size, cols), f32),
             pltpu.VMEM((2, size, cols), f32),
             pltpu.VMEM((nz, 2, size, cols), f32),

time: 44.7 us -> 40.5 us (0.906); the launches traced: 43.9 us -> 40.3 us
  Pallas kernels: 41.2 us -> 37.5 us
    pallas_call x1, Pallas kernels: 41.2 us -> 37.5 us  [apply_twice(): pl.pallas_call(functools.partial(apply_kernel, counts), in_specs=[pl.Bloc...]
where the time goes in v1:
time: 40.5 us; the launch traced here: 40.3 us
  Pallas kernels  37.5 us (93%)
  local copies, waits for them, and re-layouts  1.45 us (4%)
  between operations  1.29 us (3%)
    pallas_call x1, Pallas kernels, apply_twice(): pl.pallas_call(functools.partial(apply_kernel, counts), in_specs=[pl.Bloc...  37.5 us
    unnamed x2, local copies, waits for them, and re-layouts  1.45 us

profile of v1, /device:TPU:21, one launch (start us, length us, event | category | flops | bytes accessed | tf_op | source)
XLA Modules:
  0.0 40.3 jit_solution(12655769418448578)
XLA Ops:
  1.3 37.5 %apply_twice.1 = (f32[2,5,64,256]{3,2,1,0:T(8,128)S(1)}, f32[2,16,256]{2,1,0:T(8,128)S(1)}) custom-call(s32[1]{0:T(128)S(6)} %copy.17.count_ref, f32[128,128]{1,0:T(8,128)} %bitcast.4, f32[128,128]{1,0:T(8,128)} %bitcast.5, s32[128,128]{1,0:T(8,128)} %bitcast.6, s32[128,128]{1,0:T(8,128)} %bitcast.7, f32[2,5,64,256]{3,2,1,0:T(8,128)} %guess.1, ...), custom_call_target="tpu_custom_call" | custom-call | tf_op jit(solution)/shard_map/apply_twice/pallas_call | solution.py:878
  38.8 0.8 %copy.15 = f32[2,5,64,256]{3,2,1,0:T(8,128)} copy(f32[2,5,64,256]{3,2,1,0:T(8,128)S(1)} %get-tuple-element.2) | data formatting | bytes 1310720
  39.7 0.6 %copy.16 = f32[2,16,256]{2,1,0:T(8,128)} copy(f32[2,16,256]{2,1,0:T(8,128)S(1)} %get-tuple-element.3) | data formatting | bytes 65536

commit v2 on v1

--- a/solution.py
+++ b/solution.py
@@ -8,8 +8,9 @@
 from jax.experimental.pallas import tpu as pltpu
 from jax.sharding import PartitionSpec as P
 
-SHARES = (3, 2, 2, 1)
-FIRST = -1
+SHARES = (2, 2, 2, 2)
+EARLY = (3, 6)
+LAG = 2
 
 
 def lane_column(pack, lane, like):
@@ -602,25 +603,27 @@
     start_all(first)
 
     def early(turn):
-        if turn == groups + FIRST:
+        if turn == early_turns[0]:
             wait_receives(first)
             wait_sends(first)
             sweep(guess, 0, store_first)
             pack(middle)
             start_all(second)
-        elif turn == groups + bits - 1:
+        elif turn == early_turns[1]:
             wait_receives(second)
             sweep(middle, 1, store_second)
             for o in range(1, nz):
                 part_copy(o).start()
             wait_sends(second)
 
-    for turn in range(1, groups + bits):
+    turns = groups + 1 + LAG * (bits - 1)
+    early_turns = [min(turn, turns - 2 + order) for order, turn in enumerate(EARLY)]
+    for turn in range(1, turns):
         if turn < groups:
             bin_group(turn)
             half_copy(0, turn).start()
-        for bit in reversed(range(bits)):
-            g = turn - 1 - bit
+        for bit in range(bits):
+            g = turn - 1 - LAG * bit
             if 0 <= g < groups:
                 finish(bit, g)
         early(turn)

time: 40.5 us -> 38.3 us (0.946)
  Pallas kernels: 37.5 us -> 35.1 us
    pallas_call x1, Pallas kernels: 37.5 us -> 35.1 us  [apply_twice(): pl.pallas_call(functools.partial(apply_kernel, counts), in_specs=[pl.Bloc...]
where the time goes in v2:
time: 38.3 us; the launch traced here: 37.8 us
  Pallas kernels  35.1 us (92%)
  local copies, waits for them, and re-layouts  1.45 us (4%)
  between operations  1.29 us (3%)
    pallas_call x1, Pallas kernels, apply_twice(): pl.pallas_call(functools.partial(apply_kernel, counts), in_specs=[pl.Bloc...  35.1 us
    unnamed x2, local copies, waits for them, and re-layouts  1.45 us

profile of v2, /device:TPU:21, one launch (start us, length us, event | category | flops | bytes accessed | tf_op | source)
XLA Modules:
  0.0 37.8 jit_solution(7341463256175440984)
XLA Ops:
  1.3 35.1 %apply_twice.1 = (f32[2,5,64,256]{3,2,1,0:T(8,128)S(1)}, f32[2,16,256]{2,1,0:T(8,128)S(1)}) custom-call(s32[1]{0:T(128)S(6)} %copy.17.count_ref, f32[128,128]{1,0:T(8,128)} %bitcast.4, f32[128,128]{1,0:T(8,128)} %bitcast.5, s32[128,128]{1,0:T(8,128)} %bitcast.6, s32[128,128]{1,0:T(8,128)} %bitcast.7, f32[2,5,64,256]{3,2,1,0:T(8,128)} %guess.1, ...), custom_call_target="tpu_custom_call" | custom-call | tf_op jit(solution)/shard_map/apply_twice/pallas_call | solution.py:881
  36.4 0.8 %copy.15 = f32[2,5,64,256]{3,2,1,0:T(8,128)} copy(f32[2,5,64,256]{3,2,1,0:T(8,128)S(1)} %get-tuple-element.2) | data formatting | bytes 1310720
  37.2 0.6 %copy.16 = f32[2,16,256]{2,1,0:T(8,128)} copy(f32[2,16,256]{2,1,0:T(8,128)S(1)} %get-tuple-element.3) | data formatting | bytes 65536

commit v3 on v2

--- a/solution.py
+++ b/solution.py
@@ -9,7 +9,7 @@
 from jax.sharding import PartitionSpec as P
 
 SHARES = (2, 2, 2, 2)
-EARLY = (3, 6)
+EARLY = (3, 5)
 LAG = 2
 
 

time: 38.3 us -> 40.1 us (1.047)
  Pallas kernels: 35.1 us -> 36.9 us
    pallas_call x1, Pallas kernels: 35.1 us -> 36.9 us  [apply_twice(): pl.pallas_call(functools.partial(apply_kernel, counts), in_specs=[pl.Bloc...]
where the time goes in v3:
time: 40.1 us; the launch traced here: 39.6 us
  Pallas kernels  36.9 us (92%)
  local copies, waits for them, and re-layouts  1.45 us (4%)
  between operations  1.29 us (3%)
    pallas_call x1, Pallas kernels, apply_twice(): pl.pallas_call(functools.partial(apply_kernel, counts), in_specs=[pl.Bloc...  36.9 us
    unnamed x2, local copies, waits for them, and re-layouts  1.45 us

profile of v3, /device:TPU:21, one launch (start us, length us, event | category | flops | bytes accessed | tf_op | source)
XLA Modules:
  0.0 39.6 jit_solution(858020205799594113)
XLA Ops:
  1.3 36.9 %apply_twice.1 = (f32[2,5,64,256]{3,2,1,0:T(8,128)S(1)}, f32[2,16,256]{2,1,0:T(8,128)S(1)}) custom-call(s32[1]{0:T(128)S(6)} %copy.17.count_ref, f32[128,128]{1,0:T(8,128)} %bitcast.4, f32[128,128]{1,0:T(8,128)} %bitcast.5, s32[128,128]{1,0:T(8,128)} %bitcast.6, s32[128,128]{1,0:T(8,128)} %bitcast.7, f32[2,5,64,256]{3,2,1,0:T(8,128)} %guess.1, ...), custom_call_target="tpu_custom_call" | custom-call | tf_op jit(solution)/shard_map/apply_twice/pallas_call | solution.py:881
  38.2 0.8 %copy.15 = f32[2,5,64,256]{3,2,1,0:T(8,128)} copy(f32[2,5,64,256]{3,2,1,0:T(8,128)S(1)} %get-tuple-element.2) | data formatting | bytes 1310720
  39.0 0.6 %copy.16 = f32[2,16,256]{2,1,0:T(8,128)} copy(f32[2,16,256]{2,1,0:T(8,128)S(1)} %get-tuple-element.3) | data formatting | bytes 65536
